TPU v7x, 32 devices: a whole 2x2x4 slice. The times are simulated.
32 devices in a mesh: dp: 4 (over y, x), expert: 8 (over z, core).
Axes of the slice: x: 2, y: 2, z: 4, core: 2. Of those that a mesh axis runs over, the one named last changes fastest.
Arguments:
- tokens: bfloat16 [32768, 768], P(('dp', 'expert')), may hold values from -6 to 6
- cotangent: bfloat16 [32768, 768], P(('dp', 'expert')), may hold values from -6 to 6
- seg_start: int32 [32768], P(('dp', 'expert')), may hold values from 0 to 1023, as said below
- dispatch_slot: int32 [32768], P(('dp', 'expert')), may hold values from 0 to 2048, as said below
- ln1_gain: float32 [768], replicated, may hold values from 0.25 to 1.75
- ln1_shift: float32 [768], replicated, may hold values from -3 to 3
- w_qkv: bfloat16 [768, 2304], replicated, may hold values from -0.21875 to 0.21875
- w_attn_out: bfloat16 [768, 768], replicated, may hold values from -0.875 to 0.875
- ln2_gain: float32 [768], replicated, may hold values from 0.25 to 1.75
- ln2_shift: float32 [768], replicated, may hold values from -3 to 3
- w_in: bfloat16 [2, 768, 3072], replicated, may hold values from -0.21875 to 0.21875
- w_out: bfloat16 [2, 3072, 768], replicated, may hold values from -0.109375 to 0.109375
Outputs:
- result_out: bfloat16 [32768, 768], P(('dp', 'expert'))
- grad_tokens: float32 [32768, 768], P(('dp', 'expert'))
- grad_ln1_gain: float32 [768], replicated
- grad_ln1_shift: float32 [768], replicated
- grad_w_qkv: float32 [768, 2304], replicated
- grad_w_attn_out: float32 [768, 768], replicated
- grad_ln2_gain: float32 [768], replicated
- grad_ln2_shift: float32 [768], replicated
- grad_w_in: float32 [2, 768, 3072], P(None, None, 'expert')
- grad_w_out: float32 [2, 3072, 768], P(None, 'expert')
- expert_counts: int32 [2], replicated
Inputs may be any that keep to these rules, and one draw needn't show every extreme that they name: A row is an image row or a caption row. An image row's first 985 slots hold 5 images of 197 patches each, its other slots are padding, each padding token a segment of its own; a caption row is filled with captions. A token attends only to tokens of its own row with the same seg_start. `dispatch_slot`: slot s sends the token to the device at expert index s // 256 of its dp index, at place s % 256. Image tokens go to expert indices below 4, caption tokens to the others; no two tokens of one device share a slot; padding tokens, and only they, have s = 2048.
All inputs are finite; a program needn't handle non-finite values.
Results may differ from a plain program's by a relative error of at most 0.012.
Values may be sent and summed in bfloat16 or wider, within the bound.
No kernel may reach another device: no remote copies, remote signals or barrier semaphores. Data moves between devices by JAX's collectives and lax.ppermute only.
A program may use at most 320 MiB of HBM per device.

v0:
```python
import math
import jax
import jax.numpy as jnp
from jax import lax
from jax.sharding import PartitionSpec as P

HEADS = 12
DH = 64
FF = 3072
LEN = 1024
EPS = 1e-05
NEG = -1e30


def layer_norm(values, gain_vec, shift_vec):
    row_mean = jnp.mean(values, axis=-1, keepdims=True)
    centred = values - row_mean
    variance = jnp.mean(centred * centred, axis=-1, keepdims=True)
    return centred * lax.rsqrt(variance + EPS) * gain_vec + shift_vec


def gelu_exact(values):
    return jax.nn.gelu(values, approximate=False)


def contract_rows(first_op, second_op):
    return lax.dot_general(
        first_op, second_op, (((0,), (0,)), ((), ())), preferred_element_type=jnp.float32
    )


def contract_cols(first_op, second_op):
    return lax.dot_general(
        first_op, second_op, (((1,), (1,)), ((), ())), preferred_element_type=jnp.float32
    )


def row_pieces(qkv_b, seg_start, block_start, qblock):
    row_start = block_start // LEN * LEN
    query_rows = lax.dynamic_slice_in_dim(qkv_b, block_start, qblock, 0).reshape(
        qblock, 3, HEADS, DH
    )
    row_all = qkv_b.reshape(LEN, 3, HEADS, DH)
    seg_query = lax.dynamic_slice_in_dim(seg_start, block_start, qblock, 0)
    allowed = seg_query[:, None] == seg_start[None, :]
    score_scale = 1.0 / math.sqrt(DH)
    scores = (
        jnp.einsum(
            "qhd,khd->hqk", query_rows[:, 0], row_all[:, 1], preferred_element_type=jnp.float32
        )
        * score_scale
    )
    scores = jnp.where(allowed[None], scores, NEG)
    return (query_rows[:, 0], row_all[:, 1], row_all[:, 2], row_start, scores)


def shards(
    tokens,
    cotangent,
    seg_start,
    dispatch_slot,
    ln1_gain,
    ln1_shift,
    w_qkv,
    w_attn_out,
    ln2_gain,
    ln2_shift,
    w_in,
    w_out,
):
    tok_count = tokens.shape[0]
    feat_width = tokens.shape[1]
    n_expert = lax.axis_size("expert")
    group_size = n_expert // 2
    capacity = 2 * tok_count // n_expert
    n_slots = n_expert * capacity
    qblock = min(512, LEN)
    n_blocks = tok_count // qblock
    score_scale = 1.0 / math.sqrt(DH)
    own_expert = lax.axis_index("expert") // group_size
    inputs = tokens.astype(jnp.float32)
    normed_one, ln1_back = jax.vjp(layer_norm, inputs, ln1_gain, ln1_shift)
    normed_one_b = normed_one.astype(jnp.bfloat16)
    qkv_b = jnp.dot(normed_one_b, w_qkv, preferred_element_type=jnp.float32).astype(jnp.bfloat16)

    def forward_block(block_index):
        block_start = block_index * qblock
        queries, keys_row, values_row, row_start, scores = row_pieces(
            qkv_b, seg_start, block_start, qblock
        )
        top_score = jnp.max(scores, axis=-1, keepdims=True)
        shifted = jnp.exp(scores - top_score)
        totals = jnp.sum(shifted, axis=-1, keepdims=True)
        probs_b = (shifted / totals).astype(jnp.bfloat16)
        mixed_rows = jnp.einsum(
            "hqk,khd->qhd", probs_b, values_row, preferred_element_type=jnp.float32
        )
        return (
            mixed_rows.reshape(qblock, feat_width).astype(jnp.bfloat16),
            (top_score + jnp.log(totals))[..., 0],
        )

    mixed_blocks, lse_all = lax.map(forward_block, jnp.arange(n_blocks, dtype=jnp.int32))
    mixed_b = mixed_blocks.reshape(tok_count, feat_width)
    residual = inputs + jnp.dot(mixed_b, w_attn_out, preferred_element_type=jnp.float32)
    normed_two, ln2_back = jax.vjp(layer_norm, residual, ln2_gain, ln2_shift)
    normed_two_b = normed_two.astype(jnp.bfloat16)
    positions = jnp.arange(tok_count, dtype=jnp.int32)
    source_of = (
        jnp.full((n_slots,), tok_count, jnp.int32).at[dispatch_slot].set(positions, mode="drop")
    )
    zero_row = jnp.zeros((1, feat_width), jnp.bfloat16)
    send_rows = jnp.take(
        jnp.concatenate([normed_two_b, zero_row], axis=0), source_of, axis=0
    ).reshape(n_expert, capacity, feat_width)
    expert_in = lax.dynamic_index_in_dim(w_in, own_expert, 0, keepdims=False)
    expert_out = lax.dynamic_index_in_dim(w_out, own_expert, 0, keepdims=False)
    received = lax.all_to_all(send_rows, "expert", split_axis=0, concat_axis=0, tiled=True)
    flat_rows = received.reshape(-1, feat_width)
    hidden_pre = jnp.dot(flat_rows, expert_in, preferred_element_type=jnp.float32)
    hidden_b = gelu_exact(hidden_pre).astype(jnp.bfloat16)
    result = jnp.dot(hidden_b, expert_out, preferred_element_type=jnp.float32).astype(jnp.bfloat16)
    shape_lead = received.shape[:2]
    expert_rows_b, hidden_pre, received = (
        result.reshape(received.shape),
        hidden_pre.reshape(shape_lead + (FF,)),
        received,
    )
    returned = lax.all_to_all(expert_rows_b, "expert", split_axis=0, concat_axis=0, tiled=True)
    ffn_tok = jnp.take(
        jnp.concatenate([returned.reshape(n_slots, feat_width), zero_row], axis=0),
        dispatch_slot,
        axis=0,
    )
    result_out = (residual + ffn_tok.astype(jnp.float32)).astype(jnp.bfloat16)
    grad_out = cotangent.astype(jnp.float32)
    grad_send = jnp.take(jnp.concatenate([cotangent, zero_row], axis=0), source_of, axis=0).reshape(
        n_expert, capacity, feat_width
    )
    grad_expert = lax.all_to_all(grad_send, "expert", split_axis=0, concat_axis=0, tiled=True)
    grad_flat = grad_expert.reshape(n_slots, feat_width)
    rows_flat = received.reshape(n_slots, feat_width)
    pre_flat = hidden_pre.reshape(n_slots, FF)
    hidden_value, gelu_back = jax.vjp(gelu_exact, pre_flat)
    d_hidden = contract_cols(grad_flat, expert_out)
    d_pre_b = gelu_back(d_hidden)[0].astype(jnp.bfloat16)
    d_rows = contract_cols(d_pre_b, expert_in).astype(jnp.bfloat16)
    grad_back = lax.all_to_all(
        d_rows.reshape(n_expert, capacity, feat_width),
        "expert",
        split_axis=0,
        concat_axis=0,
        tiled=True,
    )
    d_normed_two = jnp.take(
        jnp.concatenate([grad_back.reshape(n_slots, feat_width), zero_row], axis=0),
        dispatch_slot,
        axis=0,
    ).astype(jnp.float32)
    part_in_t = contract_rows(d_pre_b, rows_flat)
    part_out = contract_rows(hidden_value.astype(jnp.bfloat16), grad_flat)
    which = (jnp.arange(2, dtype=jnp.int32) == own_expert)[:, None, None]
    padded_in = jnp.where(which, part_in_t[None], 0.0)
    padded_out = jnp.where(which, part_out[None], 0.0)
    group_in_t, group_out = (
        lax.psum_scatter(padded_in, "expert", scatter_dimension=1, tiled=True),
        lax.psum_scatter(padded_out, "expert", scatter_dimension=1, tiled=True),
    )
    summed_in_t, summed_out = (
        lax.psum(group_in_t.astype(jnp.bfloat16), "dp").astype(jnp.float32),
        lax.psum(group_out.astype(jnp.bfloat16), "dp").astype(jnp.float32),
    )
    d_resid_norm, grad_ln2_gain, grad_ln2_shift = ln2_back(d_normed_two)
    d_resid = grad_out + d_resid_norm
    d_branch_b = d_resid.astype(jnp.bfloat16)
    grad_w_attn_out = contract_rows(mixed_b, d_branch_b)
    d_mixed_b = contract_cols(d_branch_b, w_attn_out).astype(jnp.bfloat16)

    def backward_block(state_pair, inputs_block):
        key_grads, value_grads = state_pair
        block_index, lse_block = inputs_block
        block_start = block_index * qblock
        queries, keys_row, values_row, row_start, scores = row_pieces(
            qkv_b, seg_start, block_start, qblock
        )
        attn_probs = jnp.exp(scores - lse_block[:, :, None])
        grad_rows = lax.dynamic_slice_in_dim(d_mixed_b, block_start, qblock, 0).reshape(
            qblock, HEADS, DH
        )
        d_probs = jnp.einsum(
            "qhd,khd->hqk", grad_rows, values_row, preferred_element_type=jnp.float32
        )
        delta_rows = jnp.sum(attn_probs * d_probs, axis=-1, keepdims=True)
        d_scores = (attn_probs * (d_probs - delta_rows)).astype(jnp.bfloat16)
        d_query = (
            jnp.einsum("hqk,khd->qhd", d_scores, keys_row, preferred_element_type=jnp.float32)
            * score_scale
        )
        d_keys = (
            jnp.einsum("hqk,qhd->khd", d_scores, queries, preferred_element_type=jnp.float32)
            * score_scale
        )
        d_values = jnp.einsum(
            "hqk,qhd->khd",
            attn_probs.astype(jnp.bfloat16),
            grad_rows,
            preferred_element_type=jnp.float32,
        )
        old_keys = key_grads
        key_grads = old_keys + d_keys.reshape(LEN, feat_width)
        old_values = value_grads
        value_grads = old_values + d_values.reshape(LEN, feat_width)
        return ((key_grads, value_grads), d_query.reshape(qblock, feat_width))

    empty_grads = jnp.zeros((tok_count, feat_width), jnp.float32)
    (key_grads, value_grads), query_blocks = lax.scan(
        backward_block, (empty_grads, empty_grads), (jnp.arange(n_blocks, dtype=jnp.int32), lse_all)
    )
    query_grads = query_blocks.reshape(tok_count, feat_width)
    d_qkv = (
        jnp.stack([query_grads, key_grads, value_grads], axis=1)
        .reshape(tok_count, 3 * feat_width)
        .astype(jnp.bfloat16)
    )
    grad_w_qkv = contract_rows(normed_one_b, d_qkv)
    d_normed_one = contract_cols(d_qkv, w_qkv)
    d_inputs_norm, grad_ln1_gain, grad_ln1_shift = ln1_back(d_normed_one)
    grad_tokens = d_resid + d_inputs_norm
    modality = dispatch_slot // capacity // group_size
    local_counts = jnp.sum(
        (modality[:, None] == jnp.arange(2, dtype=jnp.int32)[None, :]).astype(jnp.float32), axis=0
    )
    reduced = lax.psum(
        (
            grad_w_qkv,
            grad_w_attn_out,
            grad_ln1_gain,
            grad_ln1_shift,
            grad_ln2_gain,
            grad_ln2_shift,
            local_counts,
        ),
        ("dp", "expert"),
    )
    all_counts = reduced[6]
    factor = jnp.sum(all_counts) / (2.0 * all_counts)
    grad_w_in = jnp.transpose(summed_in_t, (0, 2, 1)) * factor[:, None, None]
    grad_w_out = summed_out * factor[:, None, None]
    return (
        result_out,
        grad_tokens,
        reduced[2],
        reduced[3],
        reduced[0],
        reduced[1],
        reduced[4],
        reduced[5],
        grad_w_in,
        grad_w_out,
        all_counts.astype(jnp.int32),
    )


def solution(mesh):
    return jax.shard_map(
        shards,
        mesh=mesh,
        in_specs=(
            P(("dp", "expert"), None),
            P(("dp", "expert"), None),
            P(("dp", "expert")),
            P(("dp", "expert")),
            P(),
            P(),
            P(),
            P(),
            P(),
            P(),
            P(),
            P(),
        ),
        out_specs=(
            P(("dp", "expert"), None),
            P(("dp", "expert"), None),
            P(),
            P(),
            P(),
            P(),
            P(),
            P(),
            P(None, None, "expert"),
            P(None, "expert", None),
            P(),
        ),
        check_vma=False,
    )
```

profile of v0, /device:TPU:0, one launch (start us, length us, event | category | flops | bytes accessed | tf_op | source)
XLA Modules:
  0.0 1347.1 jit_solution(15896508103572154383)
XLA Ops:
  19.4 5.9 convolution_convert_fusion
  25.3 6.7 copy.44
  32.0 92.0 %while.27 = (s32[]{:T(128)}, bf16[2,512,768]{2,1,0:T(8,128)(2,1)}, f32[2,12,512]{2,1,0:T(8,128)}, s32[2]{0:T(128)S(1)}, s32[1024]{0:T(1024)S(1)}, /*index=5*/bf1...) while((s32[]{:T(128)}, bf16[2,512,768]{2,1,0:T(8,128)(2,1)}, ...), condition=%wide.region_5.6_spmd, body=%wide.region_2.5_spmd.sunk | while | flops 1687021568 | bytes 191465728 | solution.py:103
  35.5 12.1 fusion.114
  47.6 12.3 fusion.115
  63.0 9.9 fusion.116
  81.4 12.1 fusion.114
  93.5 12.3 fusion.115
  108.9 9.9 fusion.116
  133.4 11.7 gather_fusion.2
  145.1 11.8 gather_fusion
  161.8 6.3 all-to-all-start
  168.6 71.1 %all-to-all-done = bf16[8,256,768]{2,1,0:T(8,128)(2,1)} async-done(((bf16[8,256,768]{2,1,0:T(8,128)(2,1)}), bf16[8,256,768]{2,1,0:T(8,128)(2,1)}, u32[]{:S(2)}, u32[]{:S(2)}) %all-to-all-start) | async-done | bytes 3145760 | tf_op jit(solution)/shard_map/all_to_all | solution.py:118
  244.3 64.3 %multiply_convert_fusion.1 = (bf16[2048,3072]{1,0:T(8,128)(2,1)}, f32[2048,3072]{1,0:T(8,128)}, f32[2048,3072]{1,0:T(8,128)}) fusion(bf16[2048,768]{1,0:T(8,128)(2,1)} %bitcast.11, bf16[2,768,3072]{2,1,0:T(8,128)(2,1)} %param.30, s32[]{:T(128)S(6)} %select_n.60), kind=kOutput, calls=%fused_computation.47 | convolution fusion | flops 10072621056 | bytes 70778880 | tf_op jit(solution)/shard_map/dot_general | solution.py:120
  308.6 7.1 all-to-all-done.2
  315.8 33.4 %add_convert_fusion = bf16[2048,3072]{1,0:T(8,128)(2,1)} fusion(f32[2048,3072]{1,0:T(8,128)} %get-tuple-element.283, f32[2048,3072]{1,0:T(8,128)} %get-tuple-element.304, bf16[2048,768]{1,0:T(8,128)(2,1)} %bitcast.17, bf16[2,3072,768]{2,1,0:T(8,128)(2,1)} %param.31, s32[]{:T(128)S(6)} %select_n.60), kind=kOutput, calls=%fused_computation.46 | convolution fusion | flops 9751756800 | bytes 70778880 | tf_op jit(solution)/shard_map/dot_general | solution.py:33
  349.2 14.1 %fusion.79 = f32[3072,768]{1,0:T(8,128)S(1)} fusion(bf16[2048,3072]{1,0:T(8,128)(2,1)} %add_convert_fusion, bf16[2048,768]{1,0:T(8,128)(2,1)} %bitcast.11), kind=kOutput, calls=%fused_computation.163 | convolution fusion | flops 9663676416 | bytes 25165824 | tf_op jit(solution)/shard_map/dot_general | solution.py:27
  363.3 14.3 %fusion.80 = f32[3072,768]{1,0:T(8,128)S(1)} fusion(bf16[2048,3072]{1,0:T(8,128)(2,1)} %get-tuple-element.282, bf16[2048,768]{1,0:T(8,128)(2,1)} %bitcast.17), kind=kOutput, calls=%fused_computation.164 | convolution fusion | flops 9663676416 | bytes 25165824 | tf_op jit(solution)/shard_map/dot_general | solution.py:27
  377.6 13.1 broadcast_select_fusion
  391.4 15.5 %fusion.40 = bf16[2048,768]{1,0:T(8,128)(2,1)} fusion(bf16[2048,3072]{1,0:T(8,128)(2,1)} %add_convert_fusion, bf16[2,768,3072]{2,1,0:T(8,128)(2,1)} %param.30, s32[]{:T(128)S(6)} %select_n.60), kind=kOutput, calls=%fused_computation.92 | convolution fusion | flops 9665249280 | bytes 20447236 | tf_op jit(solution)/shard_map/dot_general | solution.py:33
  411.3 15.5 %fusion.43 = bf16[2048,768]{1,0:T(8,128)(2,1)} fusion(bf16[2048,3072]{1,0:T(8,128)(2,1)} %get-tuple-element.282, bf16[2,3072,768]{2,1,0:T(8,128)(2,1)} %param.31, s32[]{:T(128)S(6)} %select_n.60), kind=kOutput, calls=%fused_computation.93 | convolution fusion | flops 9665249280 | bytes 20447236 | tf_op jit(solution)/shard_map/dot_general | solution.py:122
  426.8 110.9 %all-to-all-done.3 = bf16[8,256,768]{2,1,0:T(8,128)(2,1)} async-done(((bf16[8,256,768]{2,1,0:T(8,128)(2,1)}), bf16[8,256,768]{2,1,0:T(8,128)(2,1)}, u32[]{:S(2)}, u32[]{:S(2)}) %all-to-all-start.3) | async-done | bytes 3145760 | tf_op jit(solution)/shard_map/all_to_all | solution.py:148
  546.8 103.8 %all-to-all-done.1 = bf16[8,256,768]{2,1,0:T(8,128)(2,1)} async-done(((bf16[8,256,768]{2,1,0:T(8,128)(2,1)}), bf16[8,256,768]{2,1,0:T(8,128)(2,1)}, u32[]{:S(2)}, u32[]{:S(2)}) %all-to-all-start.1) | async-done | bytes 3145760 | tf_op jit(solution)/shard_map/all_to_all | solution.py:129
  654.3 7.9 gather_fusion.3
  662.2 7.9 gather_fusion.1
  684.3 14.5 %reduce-scatter.5.cloned.1.call-done = f32[2,384,768]{2,1,0:T(8,128)} async-done(((f32[2,3072,768]{2,1,0:T(8,128)}), f32[2,384,768]{2,1,0:T(8,128)}) %reduce-scatter.5.cloned.1.call-update) | async-done | bytes 2359312 | tf_op jit(solution)/shard_map/reduce_scatter | solution.py:167
  701.6 198.7 %reduce-scatter.3.cloned.1.call-done = f32[2,384,768]{2,1,0:T(8,128)} async-done(((f32[2,3072,768]{2,1,0:T(8,128)}), f32[2,384,768]{2,1,0:T(8,128)}) %reduce-scatter.3.cloned.1.call-update) | async-done | bytes 2359312 | tf_op jit(solution)/shard_map/reduce_scatter | solution.py:166
  903.3 209.2 %while.28 = (s32[]{:T(128)}, f32[1024,768]{0,1:T(8,128)}, f32[1024,768]{0,1:T(8,128)}, bf16[2,512,768]{2,1,0:T(8,128)(2,1)}, s32[2]{0:T(128)S(1)}, /*index=5*/bf...) while((s32[]{:T(128)}, f32[1024,768]{0,1:T(8,128)}, ...), condition=%wide.region_13.16_spmd.clone, body=%wide.region_11.15_spmd.clone.sunk | while | flops 4126140416 | bytes 332425696 | solution.py:216
  915.7 10.3 fusion.122
  926.0 13.5 %fusion.123 = f32[12,64,1024]{2,1,0:T(8,128)} fusion(bf16[512,12,64]{0,2,1:T(8,128)(2,1)S(1)} %bitcast.171, f32[12,512,1024]{2,1,0:T(8,128)} %fusion.122, f32[12,512]{1,0:T(8,128)S(1)} %copy-done.21, pred[512,1024]{1,0:T(8,128)(4,1)S(1)} %copy-done.4), kind=kOutput, calls=%fused_computation.26.clone.1 | convolution fusion | flops 830472192 | bytes 29646848 | tf_op jit(solution)/shard_map/while/body/eval_jaxpr/hqk,qhd->khd/dot_general | solution.py:203
  939.5 18.9 %multiply_reduce_fusion.3 = (f32[12,512]{1,0:T(8,128)}, f32[12,512,1024]{2,1,0:T(8,128)}) fusion(f32[12,512,1024]{2,1,0:T(8,128)} %fusion.122, f32[12,512]{1,0:T(8,128)} %dynamic-slice_bitcast_fusion.2, pred[512,1024]{1,0:T(8,128)(4,1)} %broadcast_compare_fusion.5, bf16[512,12,64]{0,2,1:T(8,128)(2,1)} %bitcast.170, ...), kind=kOutput, calls=%fused_computation.23.clone.1 | convolution fusion | flops 836757504 | bytes 53272576 | tf_op jit(solution)/shard_map/while/body/eval_jaxpr/qhd,khd->hqk/dot_general | solution.py:190
  958.4 23.4 %multiply_convert_fusion.3 = bf16[12,512,1024]{2,1,0:T(8,128)(2,1)} fusion(f32[12,512,1024]{2,1,0:T(8,128)} %get-tuple-element.406, f32[12,512,1024]{2,1,0:T(8,128)} %fusion.122, f32[12,512]{1,0:T(8,128)} %get-tuple-element.407, f32[12,512]{1,0:T(8,128)} %dynamic-slice_bitcast_fusion.2, pred[512,1024]{1,0:T(8,128)(4,1)} %broadcast_compare_fusion.5), kind=kLoop, calls=%fused_computation.22.clone.1 | loop fusion | flops 37748736 | bytes 63488000 | tf_op jit(solution)/shard_map/while/body/eval_jaxpr/convert_element_type | solution.py:194
  981.8 9.8 convolution_multiply_fusion.5
  991.6 7.3 convolution_multiply_fusion.4
  1020.8 10.1 fusion.122
  1030.9 13.1 fusion.123
  1044.0 18.8 %multiply_reduce_fusion.3 = (f32[12,512]{1,0:T(8,128)}, f32[12,512,1024]{2,1,0:T(8,128)}) fusion(f32[12,512,1024]{2,1,0:T(8,128)} %fusion.122, f32[12,512]{1,0:T(8,128)} %dynamic-slice_bitcast_fusion.2, pred[512,1024]{1,0:T(8,128)(4,1)} %broadcast_compare_fusion.5, bf16[512,12,64]{0,2,1:T(8,128)(2,1)} %bitcast.170, ...), kind=kOutput, calls=%fused_computation.23.clone.1 | convolution fusion | flops 836757504 | bytes 53272576 | tf_op jit(solution)/shard_map/while/body/eval_jaxpr/qhd,khd->hqk/dot_general | solution.py:190
  1062.8 22.2 %multiply_convert_fusion.3 = bf16[12,512,1024]{2,1,0:T(8,128)(2,1)} fusion(f32[12,512,1024]{2,1,0:T(8,128)} %get-tuple-element.406, f32[12,512,1024]{2,1,0:T(8,128)} %fusion.122, f32[12,512]{1,0:T(8,128)} %get-tuple-element.407, f32[12,512]{1,0:T(8,128)} %dynamic-slice_bitcast_fusion.2, pred[512,1024]{1,0:T(8,128)(4,1)} %broadcast_compare_fusion.5), kind=kLoop, calls=%fused_computation.22.clone.1 | loop fusion | flops 37748736 | bytes 63488000 | tf_op jit(solution)/shard_map/while/body/eval_jaxpr/convert_element_type | solution.py:194
  1085.0 9.8 convolution_multiply_fusion.5
  1094.8 7.3 convolution_multiply_fusion.4
  1118.6 5.0 pad_maximum_fusion
  1123.6 6.6 copy.51
  1135.2 6.7 fusion.69
  1143.2 8.7 fusion.73
  1154.3 39.8 %all-reduce.4 = (f32[768]{0:T(1024)}, f32[768]{0:T(1024)}, f32[768]{0:T(1024)}, f32[768]{0:T(1024)}, f32[2]{0:T(128)}) all-reduce(f32[768]{0:T(1024)} %get-tuple-element.234, f32[768]{0:T(1024)} %get-tuple-element.238, f32[768]{0:T(1024)} %get-tuple-element.236, ...), channel_id=1, replica_groups=mesh['dp'=4,'expert'=8] {'dp','expert'}, use_global_device_ids=true, to_apply=%region_17.20 | all-reduce | flops 3074 | bytes 24592 | tf_op jit(solution)/shard_map/psum | solution.py:233
  1198.0 6.1 add_add_fusion.2
  1211.5 120.9 %all-reduce.10.cloned.1.call-done = (f32[768,2304]{1,0:T(8,128)}, f32[768,768]{1,0:T(8,128)}) async-done(((f32[768,2304]{1,0:T(8,128)}, f32[768,768]{1,0:T(8,128)}), (f32[768,2304]{1,0:T(8,128)}, f32[768,768]{1,0:T(8,128)})) %all-reduce.10.cloned.1.call-update) | async-done | bytes 9437200 | tf_op jit(solution)/shard_map/psum | solution.py:233
  1332.4 6.6 copy.110
  (238 shorter events, 161.1 us)
Async XLA Ops:
  7.2 12.2 copy-start
  7.2 12.2 copy-start.47
  13.1 6.2 copy-start.57
  14.3 5.0 copy-start.14
  25.3 6.7 copy-start.25
  47.6 15.4 %copy-start.1 = (f32[12,512,1024]{2,1,0:T(8,128)S(1)}, f32[12,512,1024]{2,1,0:T(8,128)}, u32[]{:S(2)}) copy-start(f32[12,512,1024]{2,1,0:T(8,128)} %get-tuple-element.395) | copy-start | bytes 75497472 | tf_op jit(solution)/shard_map/while
  63.0 9.9 copy-start.27
  93.5 15.4 %copy-start.1 = (f32[12,512,1024]{2,1,0:T(8,128)S(1)}, f32[12,512,1024]{2,1,0:T(8,128)}, u32[]{:S(2)}) copy-start(f32[12,512,1024]{2,1,0:T(8,128)} %get-tuple-element.395) | copy-start | bytes 75497472 | tf_op jit(solution)/shard_map/while
  108.9 9.9 copy-start.27
  145.1 11.8 copy-start.53
  161.8 78.0 %all-to-all-start = ((bf16[8,256,768]{2,1,0:T(8,128)(2,1)}), bf16[8,256,768]{2,1,0:T(8,128)(2,1)}, u32[]{:S(2)}, u32[]{:S(2)}) async-start(bf16[8,256,768]{2,1,0:T(8,128)(2,1)} %bitcast.175), calls=%async_computation | async-start | bytes 6291456 | tf_op jit(solution)/shard_map/all_to_all | solution.py:118
  239.8 76.0 %all-to-all-start.2 = ((bf16[8,256,768]{2,1,0:T(8,128)(2,1)}), bf16[8,256,768]{2,1,0:T(8,128)(2,1)}, u32[]{:S(2)}, u32[]{:S(2)}) async-start(bf16[8,256,768]{2,1,0:T(8,128)(2,1)} %bitcast.174), calls=%async_computation.2 | async-start | bytes 6291456 | tf_op jit(solution)/shard_map/all_to_all | solution.py:140
  244.2 454.6 %reduce-scatter.5.cloned.1.call-start = ((), (), s32[]{:S(2)}) async-start(), calls=%async_computation.7 | async-start | bytes 21233664 | tf_op jit(solution)/shard_map/reduce_scatter | solution.py:167
  363.3 14.3 %copy-start.55 = (pred[2]{0:T(512)(128)(4,1)S(1)}, pred[2]{0:T(512)(128)(4,1)}, u32[]{:S(2)}) copy-start(pred[2]{0:T(512)(128)(4,1)} %iota_compare_fusion) | copy-start | bytes 10
  390.7 509.7 %reduce-scatter.3.cloned.1.call-start = ((), (), s32[]{:S(2)}) async-start(), calls=%async_computation.6 | async-start | bytes 21233664 | tf_op jit(solution)/shard_map/reduce_scatter | solution.py:166
  406.9 130.8 %all-to-all-start.3 = ((bf16[8,256,768]{2,1,0:T(8,128)(2,1)}), bf16[8,256,768]{2,1,0:T(8,128)(2,1)}, u32[]{:S(2)}, u32[]{:S(2)}) async-start(bf16[8,256,768]{2,1,0:T(8,128)(2,1)} %bitcast.181), calls=%async_computation.3 | async-start | bytes 6291456 | tf_op jit(solution)/shard_map/all_to_all | solution.py:148
  537.7 4.7 copy-start.50
  537.7 112.8 %all-to-all-start.1 = ((bf16[8,256,768]{2,1,0:T(8,128)(2,1)}), bf16[8,256,768]{2,1,0:T(8,128)(2,1)}, u32[]{:S(2)}, u32[]{:S(2)}) async-start(bf16[8,256,768]{2,1,0:T(8,128)(2,1)} %bitcast.180), calls=%async_computation.1 | async-start | bytes 6291456 | tf_op jit(solution)/shard_map/all_to_all | solution.py:129
  542.4 661.7 %all-reduce.12.cloned.1.call-start = ((), (), s32[]{:S(2)}) async-start(), calls=%async_computation.9 | async-start | bytes 4718592 | tf_op jit(solution)/shard_map/psum | solution.py:170
  662.2 7.9 copy-start.30
  662.2 7.9 copy-start.35
  662.2 7.9 copy-start.43
  674.3 4.6 copy-start.18
  701.6 201.7 %copy-start.26 = (s32[1024]{0:T(1024)S(1)}, s32[1024]{0:T(1024)}, u32[]{:S(2)}) copy-start(s32[1024]{0:T(1024)} %param.22) | copy-start | bytes 12292
  903.2 429.2 %all-reduce.10.cloned.1.call-start = ((), (), s32[]{:S(2)}) async-start(), calls=%async_computation.8 | async-start | bytes 18874368 | tf_op jit(solution)/shard_map/psum | solution.py:233
  915.7 10.3 copy-start.4
  915.7 10.3 copy-start.10
  915.7 10.3 copy-start.21
  991.6 7.3 copy-start.5
  991.6 7.3 copy-start.7
  991.6 7.6 copy-start.9
  1020.8 10.1 copy-start.4
  1020.8 10.1 copy-start.10
  1020.8 10.1 copy-start.21
  1094.8 7.3 copy-start.5
  1094.8 7.3 copy-start.7
  1094.8 7.6 copy-start.9
  1130.3 4.9 copy-start.15
  1130.3 4.9 copy-start.22
  1130.3 4.9 copy-start.33
  1130.3 4.9 copy-start.37
  1130.3 4.9 copy-start.48
  1130.3 4.9 copy-start.58
  1143.2 8.7 copy-start.39
  1143.2 8.7 copy-start.16
  1143.2 8.7 copy-start.49
  1151.9 46.0 %copy-start.45 = (f32[1024]{0:T(1024)S(1)}, f32[1024]{0:T(1024)}, u32[]{:S(2)}) copy-start(f32[1024]{0:T(1024)} %copy-done.44) | copy-start | bytes 12292
  1332.4 6.6 copy-start.23
  (32 other events, 74.0 us)
Sparse Core Ops, SparseCore 0:
  390.8 307.9 reduce-scatter.4
  701.2 199.1 reduce-scatter.2
  903.5 72.5 all-reduce.11
  1142.0 190.3 all-reduce.9
where the time goes:
time: 1360 us; the launch traced here: 1350 us
  waiting for transfers between devices  628 us (46%)
  matrix products  352 us (26%)
  local copies, waits for them, and re-layouts  147 us (11%)
  other arithmetic  142 us (10%)
  blocking collectives  39.8 us (3%)
  starting transfers between devices  20 us (1%)
  between operations  14.5 us (1%)
    reduce_scatter x1, waiting for transfers between devices, shards(): lax.psum_scatter(padded_in, 'expert', scatter_dimension=1, tiled=True)  199 us
    psum x1, waiting for transfers between devices, shards(): lax.psum((grad_w_qkv, grad_w_attn_out, grad_ln1_gain, grad_ln1_shift, gra...  121 us
    all_to_all x1, waiting for transfers between devices, shards(): lax.all_to_all(d_rows.reshape(n_expert, capacity, feat_width), 'expert',...  111 us
    all_to_all x1, waiting for transfers between devices, shards(): lax.all_to_all(expert_rows_b, 'expert', split_axis=0, concat_axis=0, tile...  104 us
    all_to_all x1, waiting for transfers between devices, shards(): lax.all_to_all(send_rows, 'expert', split_axis=0, concat_axis=0, tiled=True)  71.1 us
    dot_general x1, matrix products, shards(): jnp.dot(flat_rows, expert_in, preferred_element_type=jnp.float32)  64.3 us
    dot_general x4, matrix products, contract_cols(): lax.dot_general(first_op, second_op, (((1,), (1,)), ((), ())), preferred_...  60.2 us
    convert_element_type x2, other arithmetic, backward_block(): d_scores = (attn_probs * (d_probs - delta_rows)).astype(jnp.bfloat16)  45.5 us
  transfers between devices with their start and end apart: 8, of which 7 were waited for; matrix products, arithmetic and copies ran while one was open for 29% of the time, Pallas kernels for 0%

commit v1 on v0

--- a/solution.py
+++ b/solution.py
@@ -231,16 +231,19 @@
         (modality[:, None] == jnp.arange(2, dtype=jnp.int32)[None, :]).astype(jnp.float32), axis=0
     )
     reduced = lax.psum(
-        (
-            grad_w_qkv,
-            grad_w_attn_out,
-            grad_ln1_gain,
-            grad_ln1_shift,
-            grad_ln2_gain,
-            grad_ln2_shift,
-            local_counts,
+        lax.psum(
+            (
+                grad_w_qkv,
+                grad_w_attn_out,
+                grad_ln1_gain,
+                grad_ln1_shift,
+                grad_ln2_gain,
+                grad_ln2_shift,
+                local_counts,
+            ),
+            "expert",
         ),
-        ("dp", "expert"),
+        "dp",
     )
     all_counts = reduced[6]
     factor = jnp.sum(all_counts) / (2.0 * all_counts)

time: 1360 us -> 1420 us (1.044)
  waiting for transfers between devices: 628 us -> 682 us
    reduce_scatter x1, waiting for transfers between devices: 199 us -> 0.01 us  [shards(): lax.psum_scatter(padded_in, 'expert', scatter_dimension=1, tiled=True)]
    psum x0 -> x1, waiting for transfers between devices: none -> 186 us  [shards(): lax.psum(lax.psum((grad_w_qkv, grad_w_attn_out, grad_ln1_gain, grad_ln1_s...]
    psum x1, waiting for transfers between devices: 121 us -> 192 us  [shards(): lax.psum((grad_w_qkv, grad_w_attn_out, grad_ln1_gain, grad_ln1_shift, gra...]
    psum x0 -> x1, blocking collectives: none -> 17.9 us  [shards(): lax.psum(lax.psum((grad_w_qkv, grad_w_attn_out, grad_ln1_gain, grad_ln1_s...]
    reduce_scatter x1, waiting for transfers between devices: 14.5 us -> 0.02 us  [shards(): lax.psum_scatter(padded_out, 'expert', scatter_dimension=1, tiled=True)]
  transfers between devices with their start and end apart: 8 -> 9, of which waited for: 7 -> 7; matrix products, arithmetic and copies ran while one was open for 29% -> 28% of each run, Pallas kernels for 0% -> 0%
where the time goes in v1:
time: 1420 us; the launch traced here: 1410 us
  waiting for transfers between devices  682 us (48%)
  matrix products  352 us (25%)
  local copies, waits for them, and re-layouts  147 us (10%)
  other arithmetic  141 us (10%)
  blocking collectives  47 us (3%)
  starting transfers between devices  20.1 us (1%)
  between operations  14.5 us (1%)
    psum x1, waiting for transfers between devices, shards(): lax.psum((grad_w_qkv, grad_w_attn_out, grad_ln1_gain, grad_ln1_shift, gra...  192 us
    psum x1, waiting for transfers between devices, shards(): lax.psum(lax.psum((grad_w_qkv, grad_w_attn_out, grad_ln1_gain, grad_ln1_s...  186 us
    all_to_all x1, waiting for transfers between devices, shards(): lax.all_to_all(d_rows.reshape(n_expert, capacity, feat_width), 'expert',...  111 us
    all_to_all x1, waiting for transfers between devices, shards(): lax.all_to_all(expert_rows_b, 'expert', split_axis=0, concat_axis=0, tile...  105 us
    all_to_all x1, waiting for transfers between devices, shards(): lax.all_to_all(send_rows, 'expert', split_axis=0, concat_axis=0, tiled=True)  71.1 us
    dot_general x1, matrix products, shards(): jnp.dot(flat_rows, expert_in, preferred_element_type=jnp.float32)  64.3 us
    dot_general x4, matrix products, contract_cols(): lax.dot_general(first_op, second_op, (((1,), (1,)), ((), ())), preferred_...  59.2 us
    convert_element_type x2, other arithmetic, backward_block(): d_scores = (attn_probs * (d_probs - delta_rows)).astype(jnp.bfloat16)  45 us
  transfers between devices with their start and end apart: 9, of which 7 were waited for; matrix products, arithmetic and copies ran while one was open for 28% of the time, Pallas kernels for 0%

profile of v1, /device:TPU:0, one launch (start us, length us, event | category | flops | bytes accessed | tf_op | source)
XLA Modules:
  0.0 1407.5 jit_solution(5303062303153715847)
XLA Ops:
  19.4 5.9 convolution_convert_fusion
  25.3 6.6 copy.44
  31.9 91.7 %while.27 = (s32[]{:T(128)}, bf16[2,512,768]{2,1,0:T(8,128)(2,1)}, f32[2,12,512]{2,1,0:T(8,128)}, s32[2]{0:T(128)S(1)}, s32[1024]{0:T(1024)S(1)}, /*index=5*/bf1...) while((s32[]{:T(128)}, bf16[2,512,768]{2,1,0:T(8,128)(2,1)}, ...), condition=%wide.region_5.6_spmd, body=%wide.region_2.5_spmd.sunk | while | flops 1687021568 | bytes 191465728 | solution.py:103
  35.4 12.0 fusion.114
  47.4 12.3 fusion.115
  62.8 9.9 fusion.116
  81.2 12.0 fusion.114
  93.2 12.3 fusion.115
  108.6 9.9 fusion.116
  133.1 11.7 gather_fusion.2
  144.8 11.7 gather_fusion
  161.5 6.3 all-to-all-start
  168.3 71.1 %all-to-all-done = bf16[8,256,768]{2,1,0:T(8,128)(2,1)} async-done(((bf16[8,256,768]{2,1,0:T(8,128)(2,1)}), bf16[8,256,768]{2,1,0:T(8,128)(2,1)}, u32[]{:S(2)}, u32[]{:S(2)}) %all-to-all-start) | async-done | bytes 3145760 | tf_op jit(solution)/shard_map/all_to_all | solution.py:118
  244.0 64.3 %multiply_convert_fusion.1 = (bf16[2048,3072]{1,0:T(8,128)(2,1)}, f32[2048,3072]{1,0:T(8,128)}, f32[2048,3072]{1,0:T(8,128)}) fusion(bf16[2048,768]{1,0:T(8,128)(2,1)} %bitcast.11, bf16[2,768,3072]{2,1,0:T(8,128)(2,1)} %param.30, s32[]{:T(128)S(6)} %select_n.60), kind=kOutput, calls=%fused_computation.47 | convolution fusion | flops 10072621056 | bytes 70778880 | tf_op jit(solution)/shard_map/dot_general | solution.py:120
  308.3 7.2 all-to-all-done.2
  315.4 33.1 %add_convert_fusion = bf16[2048,3072]{1,0:T(8,128)(2,1)} fusion(f32[2048,3072]{1,0:T(8,128)} %get-tuple-element.290, f32[2048,3072]{1,0:T(8,128)} %get-tuple-element.311, bf16[2048,768]{1,0:T(8,128)(2,1)} %bitcast.17, bf16[2,3072,768]{2,1,0:T(8,128)(2,1)} %param.31, s32[]{:T(128)S(6)} %select_n.60), kind=kOutput, calls=%fused_computation.46 | convolution fusion | flops 9751756800 | bytes 70778880 | tf_op jit(solution)/shard_map/dot_general | solution.py:33
  348.5 14.1 %fusion.79 = f32[3072,768]{1,0:T(8,128)S(1)} fusion(bf16[2048,3072]{1,0:T(8,128)(2,1)} %add_convert_fusion, bf16[2048,768]{1,0:T(8,128)(2,1)} %bitcast.11), kind=kOutput, calls=%fused_computation.163 | convolution fusion | flops 9663676416 | bytes 25165824 | tf_op jit(solution)/shard_map/dot_general | solution.py:27
  362.6 14.3 %fusion.80 = f32[3072,768]{1,0:T(8,128)S(1)} fusion(bf16[2048,3072]{1,0:T(8,128)(2,1)} %get-tuple-element.289, bf16[2048,768]{1,0:T(8,128)(2,1)} %bitcast.17), kind=kOutput, calls=%fused_computation.164 | convolution fusion | flops 9663676416 | bytes 25165824 | tf_op jit(solution)/shard_map/dot_general | solution.py:27
  377.0 12.8 broadcast_select_fusion
  390.5 15.5 %fusion.40 = bf16[2048,768]{1,0:T(8,128)(2,1)} fusion(bf16[2048,3072]{1,0:T(8,128)(2,1)} %add_convert_fusion, bf16[2,768,3072]{2,1,0:T(8,128)(2,1)} %param.30, s32[]{:T(128)S(6)} %select_n.60), kind=kOutput, calls=%fused_computation.92 | convolution fusion | flops 9665249280 | bytes 20447236 | tf_op jit(solution)/shard_map/dot_general | solution.py:33
  410.5 15.5 %fusion.43 = bf16[2048,768]{1,0:T(8,128)(2,1)} fusion(bf16[2048,3072]{1,0:T(8,128)(2,1)} %get-tuple-element.289, bf16[2,3072,768]{2,1,0:T(8,128)(2,1)} %param.31, s32[]{:T(128)S(6)} %select_n.60), kind=kOutput, calls=%fused_computation.93 | convolution fusion | flops 9665249280 | bytes 20447236 | tf_op jit(solution)/shard_map/dot_general | solution.py:122
  426.0 110.8 %all-to-all-done.3 = bf16[8,256,768]{2,1,0:T(8,128)(2,1)} async-done(((bf16[8,256,768]{2,1,0:T(8,128)(2,1)}), bf16[8,256,768]{2,1,0:T(8,128)(2,1)}, u32[]{:S(2)}, u32[]{:S(2)}) %all-to-all-start.3) | async-done | bytes 3145760 | tf_op jit(solution)/shard_map/all_to_all | solution.py:148
  545.9 104.9 %all-to-all-done.1 = bf16[8,256,768]{2,1,0:T(8,128)(2,1)} async-done(((bf16[8,256,768]{2,1,0:T(8,128)(2,1)}), bf16[8,256,768]{2,1,0:T(8,128)(2,1)}, u32[]{:S(2)}, u32[]{:S(2)}) %all-to-all-start.1) | async-done | bytes 3145760 | tf_op jit(solution)/shard_map/all_to_all | solution.py:129
  654.5 8.0 gather_fusion.3
  662.5 7.9 gather_fusion.1
  683.8 209.6 %while.28 = (s32[]{:T(128)}, f32[1024,768]{0,1:T(8,128)}, f32[1024,768]{0,1:T(8,128)}, bf16[2,512,768]{2,1,0:T(8,128)(2,1)}, s32[2]{0:T(128)S(1)}, /*index=5*/bf...) while((s32[]{:T(128)}, f32[1024,768]{0,1:T(8,128)}, ...), condition=%wide.region_13.16_spmd.clone, body=%wide.region_11.15_spmd.clone.sunk | while | flops 4126140416 | bytes 332425696 | solution.py:216
  696.2 10.2 fusion.122
  706.5 13.1 fusion.123
  719.5 18.8 %multiply_reduce_fusion.3 = (f32[12,512]{1,0:T(8,128)}, f32[12,512,1024]{2,1,0:T(8,128)}) fusion(f32[12,512,1024]{2,1,0:T(8,128)} %fusion.122, f32[12,512]{1,0:T(8,128)} %dynamic-slice_bitcast_fusion.2, pred[512,1024]{1,0:T(8,128)(4,1)} %broadcast_compare_fusion.5, bf16[512,12,64]{0,2,1:T(8,128)(2,1)} %bitcast.170, ...), kind=kOutput, calls=%fused_computation.23.clone.1 | convolution fusion | flops 836757504 | bytes 53272576 | tf_op jit(solution)/shard_map/while/body/eval_jaxpr/qhd,khd->hqk/dot_general | solution.py:190
  738.3 22.5 %multiply_convert_fusion.3 = bf16[12,512,1024]{2,1,0:T(8,128)(2,1)} fusion(f32[12,512,1024]{2,1,0:T(8,128)} %get-tuple-element.413, f32[12,512,1024]{2,1,0:T(8,128)} %fusion.122, f32[12,512]{1,0:T(8,128)} %get-tuple-element.414, f32[12,512]{1,0:T(8,128)} %dynamic-slice_bitcast_fusion.2, pred[512,1024]{1,0:T(8,128)(4,1)} %broadcast_compare_fusion.5), kind=kLoop, calls=%fused_computation.22.clone.1 | loop fusion | flops 37748736 | bytes 63488000 | tf_op jit(solution)/shard_map/while/body/eval_jaxpr/convert_element_type | solution.py:194
  760.8 9.9 convolution_multiply_fusion.5
  770.7 7.4 convolution_multiply_fusion.4
  800.2 10.8 fusion.122
  810.9 13.3 fusion.123
  824.3 18.9 %multiply_reduce_fusion.3 = (f32[12,512]{1,0:T(8,128)}, f32[12,512,1024]{2,1,0:T(8,128)}) fusion(f32[12,512,1024]{2,1,0:T(8,128)} %fusion.122, f32[12,512]{1,0:T(8,128)} %dynamic-slice_bitcast_fusion.2, pred[512,1024]{1,0:T(8,128)(4,1)} %broadcast_compare_fusion.5, bf16[512,12,64]{0,2,1:T(8,128)(2,1)} %bitcast.170, ...), kind=kOutput, calls=%fused_computation.23.clone.1 | convolution fusion | flops 836757504 | bytes 53272576 | tf_op jit(solution)/shard_map/while/body/eval_jaxpr/qhd,khd->hqk/dot_general | solution.py:190
  843.2 22.5 %multiply_convert_fusion.3 = bf16[12,512,1024]{2,1,0:T(8,128)(2,1)} fusion(f32[12,512,1024]{2,1,0:T(8,128)} %get-tuple-element.413, f32[12,512,1024]{2,1,0:T(8,128)} %fusion.122, f32[12,512]{1,0:T(8,128)} %get-tuple-element.414, f32[12,512]{1,0:T(8,128)} %dynamic-slice_bitcast_fusion.2, pred[512,1024]{1,0:T(8,128)(4,1)} %broadcast_compare_fusion.5), kind=kLoop, calls=%fused_computation.22.clone.1 | loop fusion | flops 37748736 | bytes 63488000 | tf_op jit(solution)/shard_map/while/body/eval_jaxpr/convert_element_type | solution.py:194
  865.6 9.9 convolution_multiply_fusion.5
  875.5 7.4 convolution_multiply_fusion.4
  904.7 6.6 copy.51
  916.2 6.7 fusion.69
  928.7 192.2 %all-reduce.13.cloned.1.call-done = (f32[768,2304]{1,0:T(8,128)}, f32[768,768]{1,0:T(8,128)}) async-done(((f32[768,2304]{1,0:T(8,128)}, f32[768,768]{1,0:T(8,128)}), (f32[768,2304]{1,0:T(8,128)}, f32[768,768]{1,0:T(8,128)})) %all-reduce.13.cloned.1.call-update) | async-done | bytes 9437200 | tf_op jit(solution)/shard_map/psum | solution.py:234
  1122.2 8.1 fusion.73
  1132.7 29.1 %all-reduce.4 = (f32[768]{0:T(1024)}, f32[768]{0:T(1024)}, f32[768]{0:T(1024)}, f32[768]{0:T(1024)}, f32[2]{0:T(128)}) all-reduce(f32[768]{0:T(1024)} %get-tuple-element.234, f32[768]{0:T(1024)} %get-tuple-element.238, f32[768]{0:T(1024)} %get-tuple-element.236, ...), channel_id=1, replica_groups=mesh['dp'=4,'expert'=8] {'expert'}, use_global_device_ids=true, to_apply=%region_17.20 | all-reduce | flops 3074 | bytes 24592 | tf_op jit(solution)/shard_map/psum | solution.py:234
  1161.8 17.9 %all-reduce.6 = (f32[768]{0:T(1024)}, f32[768]{0:T(1024)}, f32[768]{0:T(1024)}, f32[768]{0:T(1024)}, f32[2]{0:T(128)}) all-reduce(f32[768]{0:T(1024)} %get-tuple-element.271, f32[768]{0:T(1024)} %get-tuple-element.272, f32[768]{0:T(1024)} %get-tuple-element.273, ...), channel_id=1, replica_groups=mesh['dp'=4,'expert'=8] {'dp'}, use_global_device_ids=true, to_apply=%region_18.21 | all-reduce | flops 3074 | bytes 24592 | tf_op jit(solution)/shard_map/psum | solution.py:233
  1183.5 6.5 add_add_fusion.2
  1190.0 9.5 all-reduce.17.cloned.1.call-done
  1206.8 185.9 %all-reduce.15.cloned.1.call-done = (f32[768,2304]{1,0:T(8,128)}, f32[768,768]{1,0:T(8,128)}) async-done(((f32[768,2304]{1,0:T(8,128)}, f32[768,768]{1,0:T(8,128)}), (f32[768,2304]{1,0:T(8,128)}, f32[768,768]{1,0:T(8,128)})) %all-reduce.15.cloned.1.call-update) | async-done | bytes 9437200 | tf_op jit(solution)/shard_map/psum | solution.py:233
  1392.8 6.6 copy.112
  (242 shorter events, 165.7 us)
Async XLA Ops:
  7.2 12.2 copy-start
  7.2 12.2 copy-start.47
  13.1 6.2 copy-start.57
  14.3 5.0 copy-start.14
  25.3 6.6 copy-start.25
  47.4 15.4 %copy-start.1 = (f32[12,512,1024]{2,1,0:T(8,128)S(1)}, f32[12,512,1024]{2,1,0:T(8,128)}, u32[]{:S(2)}) copy-start(f32[12,512,1024]{2,1,0:T(8,128)} %get-tuple-element.402) | copy-start | bytes 75497472 | tf_op jit(solution)/shard_map/while
  62.8 9.9 copy-start.27
  93.2 15.4 %copy-start.1 = (f32[12,512,1024]{2,1,0:T(8,128)S(1)}, f32[12,512,1024]{2,1,0:T(8,128)}, u32[]{:S(2)}) copy-start(f32[12,512,1024]{2,1,0:T(8,128)} %get-tuple-element.402) | copy-start | bytes 75497472 | tf_op jit(solution)/shard_map/while
  108.6 9.9 copy-start.27
  144.8 11.7 copy-start.53
  161.5 78.0 %all-to-all-start = ((bf16[8,256,768]{2,1,0:T(8,128)(2,1)}), bf16[8,256,768]{2,1,0:T(8,128)(2,1)}, u32[]{:S(2)}, u32[]{:S(2)}) async-start(bf16[8,256,768]{2,1,0:T(8,128)(2,1)} %bitcast.175), calls=%async_computation | async-start | bytes 6291456 | tf_op jit(solution)/shard_map/all_to_all | solution.py:118
  239.4 76.0 %all-to-all-start.2 = ((bf16[8,256,768]{2,1,0:T(8,128)(2,1)}), bf16[8,256,768]{2,1,0:T(8,128)(2,1)}, u32[]{:S(2)}, u32[]{:S(2)}) async-start(bf16[8,256,768]{2,1,0:T(8,128)(2,1)} %bitcast.174), calls=%async_computation.2 | async-start | bytes 6291456 | tf_op jit(solution)/shard_map/all_to_all | solution.py:140
  243.9 679.1 %reduce-scatter.5.cloned.1.call-start = ((), (), s32[]{:S(2)}) async-start(), calls=%async_computation.7 | async-start | bytes 21233664 | tf_op jit(solution)/shard_map/reduce_scatter | solution.py:167
  362.6 14.3 %copy-start.55 = (pred[2]{0:T(512)(128)(4,1)S(1)}, pred[2]{0:T(512)(128)(4,1)}, u32[]{:S(2)}) copy-start(pred[2]{0:T(512)(128)(4,1)} %iota_compare_fusion) | copy-start | bytes 10
  389.8 536.0 %reduce-scatter.3.cloned.1.call-start = ((), (), s32[]{:S(2)}) async-start(), calls=%async_computation.6 | async-start | bytes 21233664 | tf_op jit(solution)/shard_map/reduce_scatter | solution.py:166
  406.0 130.8 %all-to-all-start.3 = ((bf16[8,256,768]{2,1,0:T(8,128)(2,1)}), bf16[8,256,768]{2,1,0:T(8,128)(2,1)}, u32[]{:S(2)}, u32[]{:S(2)}) async-start(bf16[8,256,768]{2,1,0:T(8,128)(2,1)} %bitcast.181), calls=%async_computation.3 | async-start | bytes 6291456 | tf_op jit(solution)/shard_map/all_to_all | solution.py:148
  536.8 4.7 copy-start.50
  536.8 113.9 %all-to-all-start.1 = ((bf16[8,256,768]{2,1,0:T(8,128)(2,1)}), bf16[8,256,768]{2,1,0:T(8,128)(2,1)}, u32[]{:S(2)}, u32[]{:S(2)}) async-start(bf16[8,256,768]{2,1,0:T(8,128)(2,1)} %bitcast.180), calls=%async_computation.1 | async-start | bytes 6291456 | tf_op jit(solution)/shard_map/all_to_all | solution.py:129
  541.5 579.5 %all-reduce.13.cloned.1.call-start = ((), (), s32[]{:S(2)}) async-start(), calls=%async_computation.8 | async-start | bytes 18874368 | tf_op jit(solution)/shard_map/psum | solution.py:234
  662.5 7.9 copy-start.30
  662.5 7.9 copy-start.35
  662.5 7.9 copy-start.43
  674.5 4.6 copy-start.18
  696.2 10.2 copy-start.4
  696.2 10.2 copy-start.10
  696.2 10.2 copy-start.21
  770.7 7.4 copy-start.5
  770.7 7.4 copy-start.7
  770.7 7.8 copy-start.9
  800.1 10.8 copy-start.4
  800.1 10.8 copy-start.10
  800.1 10.8 copy-start.21
  875.5 7.4 copy-start.5
  875.5 7.4 copy-start.7
  875.5 7.8 copy-start.9
  911.3 4.9 copy-start.15
  911.3 4.9 copy-start.22
  911.3 4.9 copy-start.33
  911.3 4.9 copy-start.37
  911.3 4.9 copy-start.48
  911.3 4.9 copy-start.58
  922.9 276.6 %all-reduce.17.cloned.1.call-start = ((), (), s32[]{:S(2)}) async-start(), calls=%async_computation.10 | async-start | bytes 4718592 | tf_op jit(solution)/shard_map/psum | solution.py:170
  928.6 464.1 %all-reduce.15.cloned.1.call-start = ((), (), s32[]{:S(2)}) async-start(), calls=%async_computation.9 | async-start | bytes 18874368 | tf_op jit(solution)/shard_map/psum | solution.py:233
  1122.2 8.1 copy-start.39
  1122.2 8.1 copy-start.16
  1122.2 8.1 copy-start.49
  1130.3 53.2 %copy-start.45 = (f32[1024]{0:T(1024)S(1)}, f32[1024]{0:T(1024)}, u32[]{:S(2)}) copy-start(f32[1024]{0:T(1024)} %copy-done.44) | copy-start | bytes 12292
  1392.8 6.6 copy-start.23
  (33 other events, 77.1 us)
Sparse Core Ops, SparseCore 0:
  389.9 308.6 reduce-scatter.4
  700.9 198.4 reduce-scatter.2
  923.1 197.8 all-reduce.12
  1125.0 74.4 all-reduce.16
  1203.5 189.1 all-reduce.14
